TPU v7x, 256 devices: a whole 4x4x8 slice. The times are simulated.
256 devices in a mesh: row: 16 (over z, core), col: 16 (over y, x).
Axes of the slice: x: 4, y: 4, z: 8, core: 2. Of those that a mesh axis runs over, the one named last changes fastest.
Arguments:
- inputs: bfloat16 [2048, 8192], P('col', 'row'), may hold values from -6 to 6
- weight: bfloat16 [8192, 28672], P('row', 'col'), may hold values from -0.09375 to 0.09375
- mask: int32 [64, 224], P('row', 'col'), may hold values 0 or 1
- cotangent: bfloat16 [2048, 28672], P('row', 'col'), may hold values from -6 to 6
Outputs:
- outputs: bfloat16 [2048, 28672], P('row', 'col')
- input_grad: bfloat16 [2048, 8192], P('col', 'row')
- weight_grad: bfloat16 [8192, 28672], P('row', 'col')
Inputs may be any that keep to these rules, and one draw needn't show every extreme that they name: mask holds only zeros and ones.
All inputs are finite; a program needn't handle non-finite values. No bound on the sum of `mask` on one device may be relied on, other than what follows from the above.
Results may differ from a plain program's by a relative error of at most 0.022.
Values may be sent and summed in bfloat16 or wider, within the bound.
A program may use at most 128 MiB of HBM per device.

v0:
```python
import jax
import jax.numpy as jnp
from jax import lax
from jax.sharding import PartitionSpec as P

BLOCK = 128


def expand_mask(mask_tile):
    tile_rows, tile_cols = mask_tile.shape
    mask_bf16 = mask_tile.astype(jnp.bfloat16)
    widened = jnp.broadcast_to(mask_bf16[:, None, :, None], (tile_rows, BLOCK, tile_cols, BLOCK))
    return widened.reshape(tile_rows * BLOCK, tile_cols * BLOCK)


def local(inputs, weight, mask, cotangent):
    keep_mask = expand_mask(mask)
    masked = weight * keep_mask
    whole = lax.all_gather(inputs, "col", axis=0, tiled=True)
    token_total = whole.shape[0]
    chosen = whole
    outputs = lax.psum_scatter(
        jnp.dot(chosen, masked, preferred_element_type=jnp.float32).astype(jnp.bfloat16),
        "row",
        scatter_dimension=0,
        tiled=True,
    )
    shard_rows = lax.all_gather(cotangent, "row", axis=0, tiled=True)
    partial_value = lax.dot_general(
        shard_rows, masked, (((1,), (1,)), ((), ())), preferred_element_type=jnp.float32
    )
    grad_parts = partial_value.astype(jnp.bfloat16)
    chosen = whole
    weight_acc = lax.dot_general(
        chosen, shard_rows, (((0,), (0,)), ((), ())), preferred_element_type=jnp.float32
    )
    grad_parts, weight_acc = (grad_parts, weight_acc)
    summed = lax.psum_scatter(
        grad_parts.astype(jnp.float32).astype(jnp.bfloat16), "col", scatter_dimension=0, tiled=True
    )
    grad_scale = token_total ** (-0.5)
    weight_grad = (weight_acc * keep_mask.astype(jnp.float32) * grad_scale).astype(jnp.bfloat16)
    return (outputs, summed, weight_grad)


def solution(mesh):
    placed = (P("col", "row"), P("row", "col"), P("row", "col"), P("row", "col"))
    return jax.shard_map(
        local,
        mesh=mesh,
        in_specs=placed,
        out_specs=(P("row", "col"), P("col", "row"), P("row", "col")),
        check_vma=False,
    )
```

profile of v0, /device:TPU:10, one launch (start us, length us, event | category | flops | bytes accessed | tf_op | source)
XLA Modules:
  0.0 275.3 jit_solution(2744342380747078628)
XLA Ops:
  7.2 0.0 all-gather.5.cloned.1.call-start
  7.2 0.7 all-gather.5.cloned.1.call-update
  7.9 0.0 all-gather.3.cloned.1.call-start
  7.9 0.7 all-gather.3.cloned.1.call-update
  8.6 0.0 reduce-scatter.9.cloned.1.call-start
  8.7 0.7 convert_element_type.23
  9.4 0.1 copy.14
  9.5 3.8 %copy.15 = bf16[512,1792]{0,1:T(8,128)(2,1)} copy(bf16[512,1792]{1,0:T(8,128)(2,1)} %param.5) | data formatting | bytes 3670016 | tf_op args[1]
  13.3 50.4 %all-gather.5.cloned.1.call-done = bf16[2048,1792]{1,0:T(8,128)(2,1)} async-done(((bf16[128,1792]{1,0:T(8,128)(2,1)}), bf16[2048,1792]{1,0:T(8,128)(2,1)}) %all-gather.5.cloned.1.call-update) | async-done | bytes 7340048 | tf_op jit(solution)/shard_map/all_gather | solution.py:28
  63.7 0.5 broadcast_in_dim.2
  64.2 9.1 %fusion.1 = bf16[2048,512]{0,1:T(8,128)(2,1)} fusion(bf16[2048,1792]{1,0:T(8,128)(2,1)} %all-gather.5.cloned.1.call-done, bf16[512,1792]{0,1:T(8,128)(2,1)} %copy.15, bf16[224,8,4,128]{3,2,1,0:T(4,128)(2,1)S(1)} %bitcast.23), kind=kOutput, calls=%fused_computation.4 | convolution fusion | flops 3760062464 | bytes 13107200 | tf_op jit(solution)/shard_map/dot_general | solution.py:29
  73.3 4.0 %copy.21 = bf16[2048,512]{1,0:T(8,128)(2,1)} copy(bf16[2048,512]{0,1:T(8,128)(2,1)} %fusion.1) | data formatting | bytes 4194304
  77.3 0.0 reduce-scatter.9.cloned.1.call-update
  77.3 0.2 reduce-scatter.7.cloned.1.call-start
  77.5 35.6 %all-gather.3.cloned.1.call-done = bf16[2048,512]{1,0:T(8,128)(2,1)} async-done(((bf16[128,512]{1,0:T(8,128)(2,1)}), bf16[2048,512]{1,0:T(8,128)(2,1)}) %all-gather.3.cloned.1.call-update) | async-done | bytes 2097168 | tf_op jit(solution)/shard_map/all_gather | solution.py:19
  113.1 9.1 %fusion = bf16[2048,1792]{0,1:T(8,128)(2,1)} fusion(bf16[2048,512]{1,0:T(8,128)(2,1)} %all-gather.3.cloned.1.call-done, bf16[512,1792]{0,1:T(8,128)(2,1)} %copy.15, bf16[224,8,4,128]{3,2,1,0:T(4,128)(2,1)S(1)} %bitcast.24), kind=kOutput, calls=%fused_computation.1 | convolution fusion | flops 3762683904 | bytes 13107200 | tf_op jit(solution)/shard_map/dot_general | solution.py:23
  122.2 10.1 %copy.19 = bf16[2048,1792]{1,0:T(8,128)(2,1)} copy(bf16[2048,1792]{0,1:T(8,128)(2,1)} %fusion) | data formatting | bytes 14680064
  132.3 0.0 reduce-scatter.7.cloned.1.call-update
  132.3 1.5 copy.31
  133.9 2.8 %copy.16 = bf16[512,1792]{1,0:T(8,128)(2,1)S(1)} copy(bf16[512,1792]{0,1:T(8,128)(2,1)} %bitcast.26) | data formatting | bytes 3670016 | tf_op jit(solution)/shard_map/reshape | solution.py:13
  136.7 9.1 %multiply_convert_fusion = bf16[512,1792]{1,0:T(8,128)(2,1)} fusion(bf16[512,1792]{1,0:T(8,128)(2,1)S(1)} %copy.16, bf16[2048,512]{1,0:T(8,128)(2,1)} %all-gather.3.cloned.1.call-done, bf16[2048,1792]{1,0:T(8,128)(2,1)} %all-gather.5.cloned.1.call-done), kind=kOutput, calls=%fused_computation.2 | convolution fusion | flops 3761766400 | bytes 13107200 | tf_op jit(solution)/shard_map/dot_general | solution.py:34
  145.8 50.3 %reduce-scatter.9.cloned.1.call-done = bf16[128,512]{1,0:T(8,128)(2,1)} async-done(((bf16[2048,512]{1,0:T(8,128)(2,1)}), bf16[128,512]{1,0:T(8,128)(2,1)}) %reduce-scatter.9.cloned.1.call-update) | async-done | bytes 131088
  196.1 72.7 %reduce-scatter.7.cloned.1.call-done = bf16[128,1792]{1,0:T(8,128)(2,1)} async-done(((bf16[2048,1792]{1,0:T(8,128)(2,1)}), bf16[128,1792]{1,0:T(8,128)(2,1)}) %reduce-scatter.7.cloned.1.call-update) | async-done | bytes 458768
Async XLA Ops:
  7.2 56.5 %all-gather.5.cloned.1.call-start = ((), (), s32[]{:S(2)}) async-start(), calls=%async_computation.3 | async-start | bytes 7798784 | tf_op jit(solution)/shard_map/all_gather | solution.py:28
  7.9 105.2 %all-gather.3.cloned.1.call-start = ((), (), s32[]{:S(2)}) async-start(), calls=%async_computation.2 | async-start | bytes 2228224 | tf_op jit(solution)/shard_map/all_gather | solution.py:19
  8.6 187.4 %reduce-scatter.9.cloned.1.call-start = ((), (), s32[]{:S(2)}) async-start(), calls=%async_computation.5 | async-start | bytes 2228224
  77.3 191.5 %reduce-scatter.7.cloned.1.call-start = ((), (), s32[]{:S(2)}) async-start(), calls=%async_computation.4 | async-start | bytes 7798784
Sparse Core Ops, SparseCore 0:
  9.8 53.8 all-gather.4
  66.1 46.9 all-gather.2
  117.3 78.7 reduce-scatter.8
  199.2 69.5 reduce-scatter.6
where the time goes:
time: 276 us; the launch traced here: 275 us
  waiting for transfers between devices  210 us (76%)
  matrix products  27.2 us (10%)
  local copies, waits for them, and re-layouts  22.8 us (8%)
  between operations  13.8 us (5%)
    unnamed x6, waiting for transfers between devices  124 us
    all_gather x1, waiting for transfers between devices, local(): shard_rows = lax.all_gather(cotangent, 'row', axis=0, tiled=True)  50.4 us
    all_gather x1, waiting for transfers between devices, local(): whole = lax.all_gather(inputs, 'col', axis=0, tiled=True)  35.6 us
    unnamed x4, local copies, waits for them, and re-layouts  19.4 us
    dot_general x1, matrix products, local(): jnp.dot(chosen, masked, preferred_element_type=jnp.float32)  9.1 us
    dot_general x1, matrix products, local(): lax.dot_general(chosen, shard_rows, (((0,), (0,)), ((), ())), preferred_e...  9.08 us
    dot_general x1, matrix products, local(): lax.dot_general(shard_rows, masked, (((1,), (1,)), ((), ())), preferred_e...  9.06 us
  transfers between devices with their start and end apart: 4, of which 4 were waited for; matrix products, arithmetic and copies ran while one was open for 18% of the time, Pallas kernels for 0%

commit v1 on v0

--- a/solution.py
+++ b/solution.py
@@ -16,7 +16,9 @@
 def local(inputs, weight, mask, cotangent):
     keep_mask = expand_mask(mask)
     masked = weight * keep_mask
-    whole = lax.all_gather(inputs, "col", axis=0, tiled=True)
+    whole = jnp.concatenate(
+        lax.all_to_all(jnp.stack([inputs] * lax.axis_size("col")), "col", 0, 0), axis=0
+    )
     token_total = whole.shape[0]
     chosen = whole
     outputs = lax.psum_scatter(

time: 276 us -> 226 us (0.82)
  waiting for transfers between devices: 210 us -> 152 us
  starting transfers between devices: 0.34 us -> 7.79 us
    all_gather x1, waiting for transfers between devices: 50.4 us -> 0.02 us  [local(): shard_rows = lax.all_gather(cotangent, 'row', axis=0, tiled=True)]
    all_gather x1 -> x0, waiting for transfers between devices: 35.6 us -> none  [local(): whole = lax.all_gather(inputs, 'col', axis=0, tiled=True)]
    all_to_all x0 -> x1, waiting for transfers between devices: none -> 24.4 us  [local(): lax.all_to_all(jnp.stack([inputs] * lax.axis_size('col')), 'col', 0, 0)]
    all_to_all x0 -> x1, starting transfers between devices: none -> 7.5 us  [local(): lax.all_to_all(jnp.stack([inputs] * lax.axis_size('col')), 'col', 0, 0)]
    unnamed x6 -> x5, waiting for transfers between devices: 124 us -> 127 us
    unnamed x4 -> x8, local copies, waits for them, and re-layouts: 19.4 us -> 17.9 us
  transfers between devices with their start and end apart: 4 -> 4, of which waited for: 4 -> 3; matrix products, arithmetic and copies ran while one was open for 18% -> 23% of each run, Pallas kernels for 0% -> 0%
where the time goes in v1:
time: 226 us; the launch traced here: 224 us
  waiting for transfers between devices  152 us (67%)
  matrix products  27.3 us (12%)
  local copies, waits for them, and re-layouts  23.9 us (11%)
  between operations  13.8 us (6%)
  starting transfers between devices  7.79 us (3%)
    unnamed x5, waiting for transfers between devices  127 us
    all_to_all x1, waiting for transfers between devices, local(): lax.all_to_all(jnp.stack([inputs] * lax.axis_size('col')), 'col', 0, 0)  24.4 us
    unnamed x8, local copies, waits for them, and re-layouts  17.9 us
    dot_general x1, matrix products, local(): jnp.dot(chosen, masked, preferred_element_type=jnp.float32)  9.17 us
    dot_general x1, matrix products, local(): lax.dot_general(chosen, shard_rows, (((0,), (0,)), ((), ())), preferred_e...  9.08 us
    dot_general x1, matrix products, local(): lax.dot_general(shard_rows, masked, (((1,), (1,)), ((), ())), preferred_e...  9.02 us
    all_to_all x1, starting transfers between devices, local(): lax.all_to_all(jnp.stack([inputs] * lax.axis_size('col')), 'col', 0, 0)  7.5 us
  transfers between devices with their start and end apart: 4, of which 3 were waited for; matrix products, arithmetic and copies ran while one was open for 23% of the time, Pallas kernels for 0%

profile of v1, /device:TPU:10, one launch (start us, length us, event | category | flops | bytes accessed | tf_op | source)
XLA Modules:
  0.0 224.4 jit_solution(13945207822689283063)
XLA Ops:
  7.2 0.0 all-gather.2.cloned.1.call-start
  7.2 0.7 all-gather.2.cloned.1.call-update
  7.9 2.5 %stack.2 = bf16[16,128,512]{2,1,0:T(8,128)(2,1)} broadcast(bf16[128,512]{1,0:T(8,128)(2,1)} %param.4), dimensions={1,2} | broadcast | bytes 2228224 | tf_op jit(solution)/shard_map/stack | solution.py:20
  10.4 0.0 copy-start.1
  10.4 0.0 copy-start
  10.4 7.5 %all-to-all-start = ((bf16[16,128,512]{2,1,0:T(8,128)(2,1)}), bf16[16,128,512]{2,1,0:T(8,128)(2,1)}, u32[]{:S(2)}, u32[]{:S(2)}) async-start(bf16[16,128,512]{2,1,0:T(8,128)(2,1)} %stack.2), calls=%async_computation | async-start | bytes 4194304 | tf_op jit(solution)/shard_map/all_to_all | solution.py:20
  17.9 0.0 reduce-scatter.7.cloned.1.call-start
  17.9 0.0 copy-done.1
  18.0 0.1 copy.14
  18.1 0.0 copy-done
  18.1 2.3 %copy.15 = bf16[512,1792]{0,1:T(8,128)(2,1)} copy(bf16[512,1792]{1,0:T(8,128)(2,1)S(1)} %copy-done) | data formatting | bytes 3670016 | tf_op args[1]
  20.4 24.4 %all-to-all-done = bf16[16,128,512]{2,1,0:T(8,128)(2,1)} async-done(((bf16[16,128,512]{2,1,0:T(8,128)(2,1)}), bf16[16,128,512]{2,1,0:T(8,128)(2,1)}, u32[]{:S(2)}, u32[]{:S(2)}) %all-to-all-start) | async-done | bytes 2097184 | tf_op jit(solution)/shard_map/all_to_all | solution.py:20
  44.7 0.5 broadcast_in_dim.2
  45.3 9.2 %fusion = bf16[2048,1792]{0,1:T(8,128)(2,1)} fusion(bf16[2048,512]{1,0:T(8,128)(2,1)} %bitcast, bf16[512,1792]{0,1:T(8,128)(2,1)} %copy.15, bf16[224,8,4,128]{3,2,1,0:T(4,128)(2,1)S(1)} %bitcast.24), kind=kOutput, calls=%fused_computation.1 | convolution fusion | flops 3762683904 | bytes 13107200 | tf_op jit(solution)/shard_map/dot_general | solution.py:25
  54.5 10.1 %copy.19 = bf16[2048,1792]{1,0:T(8,128)(2,1)} copy(bf16[2048,1792]{0,1:T(8,128)(2,1)} %fusion) | data formatting | bytes 14680064
  64.6 0.0 reduce-scatter.7.cloned.1.call-update
  64.6 0.2 reduce-scatter.9.cloned.1.call-start
  64.9 0.0 all-gather.2.cloned.1.call-done
  64.9 9.0 %fusion.1 = bf16[2048,512]{0,1:T(8,128)(2,1)} fusion(bf16[2048,1792]{1,0:T(8,128)(2,1)} %all-gather.2.cloned.1.call-done, bf16[512,1792]{0,1:T(8,128)(2,1)} %copy.15, bf16[224,8,4,128]{3,2,1,0:T(4,128)(2,1)S(1)} %bitcast.25), kind=kOutput, calls=%fused_computation.4 | convolution fusion | flops 3760062464 | bytes 13107200 | tf_op jit(solution)/shard_map/dot_general | solution.py:31
  73.9 3.9 %copy.21 = bf16[2048,512]{1,0:T(8,128)(2,1)} copy(bf16[2048,512]{0,1:T(8,128)(2,1)} %fusion.1) | data formatting | bytes 4194304
  77.8 0.0 reduce-scatter.9.cloned.1.call-update
  77.9 1.5 copy.31
  79.4 2.8 %copy.16 = bf16[512,1792]{1,0:T(8,128)(2,1)S(1)} copy(bf16[512,1792]{0,1:T(8,128)(2,1)} %bitcast.27) | data formatting | bytes 3670016 | tf_op jit(solution)/shard_map/reshape | solution.py:13
  82.3 9.1 %multiply_convert_fusion = bf16[512,1792]{1,0:T(8,128)(2,1)} fusion(bf16[512,1792]{1,0:T(8,128)(2,1)S(1)} %copy.16, bf16[2048,512]{1,0:T(8,128)(2,1)} %bitcast, bf16[2048,1792]{1,0:T(8,128)(2,1)} %all-gather.2.cloned.1.call-done), kind=kOutput, calls=%fused_computation.2 | convolution fusion | flops 3761766400 | bytes 13107200 | tf_op jit(solution)/shard_map/dot_general | solution.py:36
  91.3 45.9 %reduce-scatter.7.cloned.1.call-done = bf16[128,1792]{1,0:T(8,128)(2,1)} async-done(((bf16[2048,1792]{1,0:T(8,128)(2,1)}), bf16[128,1792]{1,0:T(8,128)(2,1)}) %reduce-scatter.7.cloned.1.call-update) | async-done | bytes 458768
  137.3 80.6 %reduce-scatter.9.cloned.1.call-done = bf16[128,512]{1,0:T(8,128)(2,1)} async-done(((bf16[2048,512]{1,0:T(8,128)(2,1)}), bf16[128,512]{1,0:T(8,128)(2,1)}) %reduce-scatter.9.cloned.1.call-update) | async-done | bytes 131088
  (1 shorter events, 0.0 us)
Async XLA Ops:
  7.2 57.7 %all-gather.2.cloned.1.call-start = ((), (), s32[]{:S(2)}) async-start(), calls=%async_computation.3 | async-start | bytes 7798784 | tf_op jit(solution)/shard_map/all_gather | solution.py:30
  10.4 7.5 %copy-start.1 = (s32[4,14]{1,0:T(4,128)S(1)}, s32[4,14]{1,0:T(4,128)}, u32[]{:S(2)}) copy-start(s32[4,14]{1,0:T(4,128)} %param.6) | copy-start | bytes 676
  10.4 7.7 %copy-start = (bf16[512,1792]{1,0:T(8,128)(2,1)S(1)}, bf16[512,1792]{1,0:T(8,128)(2,1)}, u32[]{:S(2)}) copy-start(bf16[512,1792]{1,0:T(8,128)(2,1)} %param.5) | copy-start | bytes 5505028
  10.4 34.4 %all-to-all-start = ((bf16[16,128,512]{2,1,0:T(8,128)(2,1)}), bf16[16,128,512]{2,1,0:T(8,128)(2,1)}, u32[]{:S(2)}, u32[]{:S(2)}) async-start(bf16[16,128,512]{2,1,0:T(8,128)(2,1)} %stack.2), calls=%async_computation | async-start | bytes 4194304 | tf_op jit(solution)/shard_map/all_to_all | solution.py:20
  17.9 119.4 %reduce-scatter.7.cloned.1.call-start = ((), (), s32[]{:S(2)}) async-start(), calls=%async_computation.4 | async-start | bytes 7798784
  64.6 153.3 %reduce-scatter.9.cloned.1.call-start = ((), (), s32[]{:S(2)}) async-start(), calls=%async_computation.5 | async-start | bytes 2228224
Sparse Core Ops, SparseCore 0:
  9.8 53.8 all-gather.1
  66.8 70.3 reduce-scatter.6
  141.4 76.4 reduce-scatter.8
